TPU v7x, 256 devices: a whole 4x4x8 slice. The times are simulated.
256 devices in a mesh: tm: 8 (over z_hi, x), space: 32 (over y, z_lo, core).
Axes of the slice: x: 4, y: 4, z: 8 (z_hi: 2, z_lo: 4; z = z_hi * 4 + z_lo), core: 2. Of those that a mesh axis runs over, the one named last changes fastest.
Arguments:
- eof_basis: bfloat16 [262144, 256], P('space'), may hold values from -0.01171875 to 0.01171875
- snapshots: bfloat16 [262144, 512], P('space', 'tm'), may hold values from -6 to 6
- inverse_energy: float32 [256], replicated, may hold values from 0.022097087 to 0.22097087
- eigen_vectors: bfloat16 [256, 512], replicated, may hold values from -0.375 to 0.375
Outputs:
- reduced_operator: float32 [256, 256], replicated
- rebuilt_modes: bfloat16 [512, 262144], P('tm', 'space')
All inputs are finite; a program needn't handle non-finite values.
Results may differ from a plain program's by a relative error of at most 0.0049.
Values may be sent and summed in bfloat16 or wider, within the bound.
A program may use at most 64 MiB of HBM per device.

v0:
```python
import jax
import jax.numpy as jnp
from jax import lax
from jax.sharding import PartitionSpec as P


def passed_along(block, axis, distance):
    devices = range(lax.axis_size(axis))
    route = [(i - distance, i) for i in devices if i - distance in devices]
    return lax.ppermute(block, axis, route)


def per_device(eof_basis, snapshots, inverse_energy, eigen_vectors):
    partial_value = lax.dot_general(
        eof_basis, snapshots, (((0,), (0,)), ((), ())), preferred_element_type=jnp.float32
    )
    coeffs = lax.psum(partial_value, "space")
    previous = passed_along(coeffs[:, -1:], "tm", 1)
    lagged = jnp.concatenate([previous, coeffs[:, :-1]], axis=1)
    scaled = lagged * inverse_energy[:, None]
    local_part = jnp.dot(coeffs, scaled.T, precision=lax.Precision.HIGHEST)
    reduced_operator = lax.psum(local_part, "tm")
    hour_weights = jnp.dot(
        scaled.T, eigen_vectors.astype(jnp.float32), precision=lax.Precision.HIGHEST
    ).astype(jnp.bfloat16)
    rebuilt = lax.psum_scatter(
        lax.dot_general(
            hour_weights, snapshots, (((0,), (1,)), ((), ())), preferred_element_type=jnp.float32
        ),
        "tm",
        scatter_dimension=0,
        tiled=True,
    )
    return (reduced_operator, rebuilt.astype(jnp.bfloat16))


def solution(mesh):
    in_specs = (P("space", None), P("space", "tm"), P(), P())
    out_specs = (P(), P("tm", "space"))
    return jax.shard_map(
        per_device, mesh=mesh, in_specs=in_specs, out_specs=out_specs, check_vma=False
    )
```

profile of v0, /device:TPU:1, one launch (start us, length us, event | category | flops | bytes accessed | tf_op | source)
XLA Modules:
  0.0 724.7 jit_solution(18432330371849172905)
XLA Ops:
  7.2 0.0 copy-start
  7.2 0.0 copy-start.3
  7.2 0.0 copy-start.2
  7.2 0.0 all-reduce.3.cloned.1.call-start
  7.2 1.1 copy-done
  8.4 3.6 fusion.6
  12.0 0.0 all-reduce.3.cloned.1.call-update
  12.0 0.0 reduce-scatter.2.cloned.1.call-start
  12.1 248.6 %all-reduce.3.cloned.1.call-done = f32[256,64]{0,1:T(8,128)} async-done(((f32[256,64]{0,1:T(8,128)}), f32[256,64]{0,1:T(8,128)}) %all-reduce.3.cloned.1.call-update) | async-done | bytes 65552 | tf_op jit(solution)/shard_map/psum | solution.py:17
  260.7 0.7 slice.8
  261.4 3.1 collective-permute-start
  264.5 0.7 collective-permute-done
  265.2 0.0 copy-done.3
  265.2 0.0 copy-done.2
  265.2 1.1 convolution_convert_fusion
  266.3 8.1 %fusion.5 = f32[512,8192]{1,0:T(8,128)} fusion(bf16[64,512]{1,0:T(8,128)(2,1)S(1)} %convolution_convert_fusion, bf16[8192,64]{0,1:T(8,128)(2,1)S(1)} %copy-done), kind=kOutput, calls=%fused_computation.7 | convolution fusion | flops 536870912 | bytes 17891328 | tf_op jit(solution)/shard_map/dot_general | solution.py:27
  274.4 0.0 copy-start.1
  274.4 0.0 reduce-scatter.2.cloned.1.call-update
  274.4 0.0 all-reduce.5.cloned.1.call-start
  274.5 0.8 copy-done.1
  275.2 1.1 fusion
  276.4 0.0 all-reduce.5.cloned.1.call-update
  276.4 323.5 %reduce-scatter.2.cloned.1.call-done = f32[64,8192]{1,0:T(8,128)} async-done(((f32[512,8192]{1,0:T(8,128)}), f32[64,8192]{1,0:T(8,128)}) %reduce-scatter.2.cloned.1.call-update) | async-done | bytes 2097168 | tf_op jit(solution)/shard_map/reduce_scatter | solution.py:26
  599.9 2.7 convert_element_type.8
  602.6 113.9 %all-reduce.5.cloned.1.call-done = f32[256,256]{1,0:T(8,128)} async-done(((f32[256,256]{1,0:T(8,128)}), f32[256,256]{1,0:T(8,128)}) %all-reduce.5.cloned.1.call-update) | async-done | bytes 262160 | tf_op jit(solution)/shard_map/psum | solution.py:22
  716.5 1.7 copy.8
Async XLA Ops:
  7.2 1.2 copy-start
  7.2 258.0 %copy-start.3 = (f32[256]{0:T(256)S(1)}, f32[256]{0:T(256)}, u32[]{:S(2)}) copy-start(f32[256]{0:T(256)} %param.6) | copy-start | bytes 3076
  7.2 258.0 %copy-start.2 = (bf16[256,512]{1,0:T(8,128)(2,1)S(1)}, bf16[256,512]{1,0:T(8,128)(2,1)}, u32[]{:S(2)}) copy-start(bf16[256,512]{1,0:T(8,128)(2,1)} %param.7) | copy-start | bytes 786436
  7.2 253.5 %all-reduce.3.cloned.1.call-start = ((), (), s32[]{:S(2)}) async-start(), calls=%async_computation.1 | async-start | bytes 131072 | tf_op jit(solution)/shard_map/psum | solution.py:17
  12.0 587.9 %reduce-scatter.2.cloned.1.call-start = ((), (), s32[]{:S(2)}) async-start(), calls=%async_computation.3 | async-start | bytes 18874368 | tf_op jit(solution)/shard_map/reduce_scatter | solution.py:26
  261.4 3.8 collective-permute-start
  274.4 0.8 copy-start.1
  274.4 442.1 %all-reduce.5.cloned.1.call-start = ((), (), s32[]{:S(2)}) async-start(), calls=%async_computation.2 | async-start | bytes 524288 | tf_op jit(solution)/shard_map/psum | solution.py:22
Sparse Core Ops, SparseCore 0:
  12.2 248.5 all-reduce.2
  274.6 325.3 reduce-scatter.1
  603.1 113.3 all-reduce.4
where the time goes:
time: 730 us; the launch traced here: 725 us
  waiting for transfers between devices  687 us (94%)
  matrix products  13.9 us (2%)
  between operations  13.8 us (2%)
    reduce_scatter x1, waiting for transfers between devices, per_device(): lax.psum_scatter(lax.dot_general(hour_weights, snapshots, (((0,), (1,)),...  324 us
    psum x1, waiting for transfers between devices, per_device(): coeffs = lax.psum(partial_value, 'space')  249 us
    psum x1, waiting for transfers between devices, per_device(): reduced_operator = lax.psum(local_part, 'tm')  114 us
  transfers between devices with their start and end apart: 4, of which 4 were waited for; matrix products, arithmetic and copies ran while one was open for 1% of the time, Pallas kernels for 0%

commit v1 on v0

v1 whole, which is shorter than its diff:
```python
import functools

import jax
import jax.numpy as jnp
from jax import lax
from jax.experimental import pallas as pl
from jax.experimental.pallas import tpu as pltpu
from jax.sharding import PartitionSpec as P

MESH = pl.DeviceIdType.MESH
F32, BF16 = jnp.float32, jnp.bfloat16

NX, NY, NZ, NZL, NCORE = 4, 4, 8, 4, 2
CHUNKS = 4
K_CHUNKS = 4
PRODUCT = (((1,), (0,)), ((), ()))
ALONG_LAST = (((1,), (1,)), ((), ()))
ALONG_FIRST = (((0,), (0,)), ((), ()))


def dot(a, b, dims=PRODUCT):
    return lax.dot_general(a, b, dims, preferred_element_type=F32)


def two_parts(a):
    high = a.astype(BF16)
    return high, (a - high.astype(F32)).astype(BF16)


def kernel(
    eof, snap, energy, vectors, operator, modes,
    eof_v, snap_v, vec_v, vec_t, parts, from_plane, from_column, total, coeffs,
    gathered, weights, rebuilt, operator_v, energy_v,
    load_sem, store_sem, send_sem, plane_sem, column_sem, x_sem, y_sem, core_sem,
    snap_sem, modes_sem,
):
    tm, space = lax.axis_index("tm"), lax.axis_index("space")
    zh, x = tm // NX, tm % NX
    y, zl, core = space // 8, (space // 2) % NZL, space % 2
    z = zh * NZL + zl
    hours, cells = snap.shape
    rank = eof.shape[1]
    piece = cells // 8
    width = piece // CHUNKS
    depth = cells // K_CHUNKS

    def at(x_, y_, z_, core_):
        return ((z_ // NZL) * NX + x_, y_ * 8 + (z_ % NZL) * 2 + core_)

    mine = y * 2 + core
    plane = [(mine + d) % 8 for d in range(1, 8)]
    plane_peers = [at(x, q // 2, z, q % 2) for q in plane]
    column_peers = [at(x, y, (z + d) % NZ, core) for d in range(1, NZ)]
    x_peers = [at((x + d) % NX, y, z, core) for d in range(1, NX)]
    y_peers = [at(x, (y + d) % NY, z, core) for d in range(1, NY)]
    other_core = at(x, y, z, 1 - core)
    far_peers = [at((x + d) % NX, y, (z + 2 + 4 * s) % NZ, core) for d in range(1, NX) for s in range(2)]

    barrier = pltpu.get_barrier_semaphore()
    peers = plane_peers + column_peers + x_peers + far_peers
    for peer in peers:
        pl.semaphore_signal(barrier, inc=1, device_id=peer, device_id_type=MESH)

    def load(source, target, i):
        copy = pltpu.make_async_copy(source, target, load_sem.at[i])
        copy.start()
        return copy

    snap_load = load(snap, snap_v, 0)
    eof_loads = [
        load(eof.at[pl.ds(k * depth, depth), :], eof_v.at[pl.ds(k * depth, depth), :], 1 + k)
        for k in range(K_CHUNKS)
    ]
    vec_load = load(vectors, vec_v, 1 + K_CHUNKS)
    energy_load = load(energy, energy_v, 2 + K_CHUNKS)

    sent = []

    def send(source, target, receive, peer, i):
        copy = pltpu.make_async_remote_copy(
            src_ref=source, dst_ref=target, send_sem=send_sem.at[i], recv_sem=receive,
            device_id=peer, device_id_type=MESH,
        )
        copy.start()
        sent.append(copy)

    def arrived(ref, sem):
        pltpu.make_async_copy(ref, ref, sem).wait()

    def send_snapshots(c):
        for d in range(NX):
            for s in range(2):
                x_, z_ = (x + d) % NX, (zl + 2 + 4 * s) % NZ
                start = pl.multiple_of((x_ * 2 + s) * piece + c * width, width)
                send(
                    snap.at[:, pl.ds(start, width)],
                    gathered.at[c, pl.ds(pl.multiple_of(tm * hours, hours), hours), :],
                    snap_sem.at[c], at(x_, y, z_, core), len(sent),
                )

    def project(k):
        eof_loads[k].wait()
        return dot(snap_v[:, k * depth:(k + 1) * depth], eof_v[k * depth:(k + 1) * depth, :])

    snap_load.wait()
    partial = project(0)
    partial += project(1)
    pl.semaphore_wait(barrier, len(peers))
    send_snapshots(0)
    for k in range(2, K_CHUNKS):
        partial += project(k)
    for q in range(8):
        parts[q] = partial[q * 8:(q + 1) * 8, :]

    for q, peer in zip(plane, plane_peers):
        send(parts.at[q], from_plane.at[mine], plane_sem, peer, len(sent))
    from_plane[mine] = parts[mine]
    vec_load.wait()
    vec_t[...] = vec_v[...].T
    arrived(from_plane.at[pl.ds(0, 7)], plane_sem)
    value = from_plane[0]
    for q in range(1, 8):
        value += from_plane[q]

    total[...] = value
    for peer in column_peers:
        send(total, from_column.at[z], column_sem, peer, len(sent))
    send_snapshots(1)
    from_column[z] = value
    arrived(from_column.at[pl.ds(0, 7)], column_sem)
    for h in range(2):
        value = from_column[h * NZL]
        for i in range(1, NZL):
            value += from_column[h * NZL + i]
        coeffs[core, y, x, h] = value

    for peer in x_peers:
        send(coeffs.at[core, y, x], coeffs.at[core, y, x], x_sem, peer, len(sent))
    send_snapshots(2)
    send_snapshots(3)
    arrived(coeffs.at[0, 0, pl.ds(0, 3)], x_sem)
    for peer in y_peers:
        send(coeffs.at[core, y], coeffs.at[core, y], y_sem, peer, len(sent))
    arrived(coeffs.at[0, pl.ds(0, 3)], y_sem)
    send(coeffs.at[core], coeffs.at[core], core_sem, other_core, len(sent))
    arrived(coeffs.at[0], core_sem)

    rows = [
        coeffs[c_, y_, x_, h]
        for h in range(2) for x_ in range(NX) for y_ in range(NY) for c_ in range(NCORE)
    ]
    whole = jnp.concatenate(rows, axis=0)
    first = lax.broadcasted_iota(jnp.int32, whole.shape, 0) == 0
    energy_load.wait()
    scaled = jnp.where(first, 0.0, pltpu.roll(whole, 1, 0)) * energy_v[...]
    scaled_high, scaled_low = two_parts(scaled)
    weights[...] = (
        dot(vec_t[...], scaled_high, ALONG_LAST) + dot(vec_t[...], scaled_low, ALONG_LAST)
    ).astype(BF16)

    owner_zl = (z + 2) % NZL
    side = ((z + 6 - owner_zl) % NZ) // 4
    owner_space = y * 8 + owner_zl * 2 + core
    for c in range(CHUNKS):
        arrived(gathered.at[c], snap_sem.at[c])
        rebuilt[c] = dot(weights[...], gathered[c]).astype(BF16)
        start = pl.multiple_of((x * 2 + side) * piece + c * width, width)
        for d in range(8):
            to = (tm + d) % 8
            send(
                rebuilt.at[c, pl.ds(pl.multiple_of(to * hours, hours), hours), :],
                modes.at[:, pl.ds(start, width)],
                modes_sem, (to, owner_space), len(sent),
            )

    whole_high, whole_low = two_parts(whole)
    operator_v[...] = (
        dot(whole_high, scaled_high, ALONG_FIRST)
        + dot(whole_high, scaled_low, ALONG_FIRST)
        + dot(whole_low, scaled_high, ALONG_FIRST)
    )
    store = pltpu.make_async_copy(operator_v, operator, store_sem)
    store.start()

    for copy in sent:
        copy.wait_send()
    store.wait()
    arrived(modes, modes_sem)


def per_device(eof_basis, snapshots, inverse_energy, eigen_vectors):
    cells, rank = eof_basis.shape
    hours = snapshots.shape[1]
    all_modes = eigen_vectors.shape[1]
    piece = cells // 8
    width = piece // CHUNKS
    anywhere = pl.BlockSpec(memory_space=pl.ANY)
    sends = 8 * CHUNKS * 2 + 7 + 7 + 3 + 3 + 1
    return pl.pallas_call(
        kernel,
        out_shape=(
            jax.ShapeDtypeStruct((rank, rank), F32),
            jax.ShapeDtypeStruct((hours, cells), BF16),
        ),
        in_specs=[anywhere] * 4,
        out_specs=(anywhere, anywhere),
        scratch_shapes=[
            pltpu.VMEM((cells, rank), BF16),
            pltpu.VMEM((hours, cells), BF16),
            pltpu.VMEM((rank, all_modes), BF16),
            pltpu.VMEM((all_modes, rank), BF16),
            pltpu.VMEM((8, 8, rank), F32),
            pltpu.VMEM((8, 8, rank), F32),
            pltpu.VMEM((NZ, 8, rank), F32),
            pltpu.VMEM((8, rank), F32),
            pltpu.VMEM((NCORE, NY, NX, 2, 8, rank), F32),
            pltpu.VMEM((CHUNKS, 8 * hours, width), BF16),
            pltpu.VMEM((all_modes, 8 * hours), BF16),
            pltpu.VMEM((CHUNKS, all_modes, width), BF16),
            pltpu.VMEM((rank, rank), F32),
            pltpu.VMEM((1, rank), F32),
            pltpu.SemaphoreType.DMA((3 + K_CHUNKS,)),
            pltpu.SemaphoreType.DMA,
            pltpu.SemaphoreType.DMA((sends,)),
            pltpu.SemaphoreType.DMA,
            pltpu.SemaphoreType.DMA,
            pltpu.SemaphoreType.DMA,
            pltpu.SemaphoreType.DMA,
            pltpu.SemaphoreType.DMA,
            pltpu.SemaphoreType.DMA((CHUNKS,)),
            pltpu.SemaphoreType.DMA,
        ],
        compiler_params=pltpu.CompilerParams(
            collective_id=0, has_side_effects=True, vmem_limit_bytes=60 * 1024 * 1024
        ),
    )(eof_basis, snapshots.T, inverse_energy.reshape(1, rank), eigen_vectors)


def solution(mesh):
    in_specs = (P("space", None), P("space", "tm"), P(), P())
    out_specs = (P(), P("tm", "space"))
    return jax.shard_map(
        per_device, mesh=mesh, in_specs=in_specs, out_specs=out_specs, check_vma=False
    )
```

time: 730 us -> 65.2 us (0.09)
  the two profiles are of different devices: /device:TPU:1 before, /device:TPU:7 now
where the time goes in v1:
time: 65.2 us; the launch traced here: 65.1 us
  Pallas kernels  60.5 us (93%)
  local copies, waits for them, and re-layouts  3.93 us (6%)
    pallas_call x1, Pallas kernels, per_device(): pl.pallas_call(kernel, out_shape=(jax.ShapeDtypeStruct((rank, rank), F32)...  60.5 us
    unnamed x2, local copies, waits for them, and re-layouts  3.93 us

profile of v1, /device:TPU:7, one launch (start us, length us, event | category | flops | bytes accessed | tf_op | source)
XLA Modules:
  0.0 65.1 jit_solution(361237309109399876)
XLA Ops:
  0.6 60.5 %shard_map.59 = (f32[256,256]{1,0:T(8,128)}, bf16[64,8192]{1,0:T(8,128)(2,1)}) custom-call(bf16[8192,256]{1,0:T(8,128)(2,1)} %eof.1, bf16[64,8192]{1,0:T(8,128)(2,1)} %bitcast.2, f32[1,256]{1,0:T(1,128)} %bitcast.3, bf16[256,512]{1,0:T(8,128)(2,1)} %vectors.1), custom_call_target="tpu_custom_call" | custom-call | tf_op jit(solution)/shard_map/pallas_call | solution.py:199
  61.2 1.7 %copy.8 = f32[256,256]{1,0:T(8,128)} copy(f32[256,256]{1,0:T(8,128)} %get-tuple-element.4) | data formatting | bytes 524288
  62.8 2.3 %copy.9 = bf16[64,8192]{1,0:T(8,128)(2,1)} copy(bf16[64,8192]{1,0:T(8,128)(2,1)} %get-tuple-element.5) | data formatting | bytes 2097152

commit v2 on v1

v2 whole, which is shorter than its diff:
```python
import functools

import jax
import jax.numpy as jnp
from jax import lax
from jax.experimental import pallas as pl
from jax.experimental.pallas import tpu as pltpu
from jax.sharding import PartitionSpec as P

MESH = pl.DeviceIdType.MESH
F32, BF16 = jnp.float32, jnp.bfloat16

NX, NY, NZ, NZL, NCORE = 4, 4, 8, 4, 2
CHUNKS = 4
K_CHUNKS = 4
PRODUCT = (((1,), (0,)), ((), ()))
ALONG_LAST = (((1,), (1,)), ((), ()))
ALONG_FIRST = (((0,), (0,)), ((), ()))


def dot(a, b, dims=PRODUCT):
    return lax.dot_general(a, b, dims, preferred_element_type=F32)


def two_parts(a):
    high = a.astype(BF16)
    return high, (a - high.astype(F32)).astype(BF16)


def kernel(
    eof, snap, energy, vectors, operator, modes,
    eof_v, snap_v, vec_v, vec_t, parts, from_plane, from_column, total, coeffs,
    gathered, weights, rebuilt, energy_v,
    load_sem, sent_sem, plane_sem, column_sem, x_sem, y_sem, core_sem,
    snap_sem, modes_sem,
):
    hours, cells = snap.shape
    piece = cells // 8
    width = piece // CHUNKS
    depth = cells // K_CHUNKS

    def load(source, target, i):
        copy = pltpu.make_async_copy(source, target, load_sem.at[i])
        copy.start()
        return copy

    snap_load = load(snap, snap_v, 0)
    eof_loads = [
        load(eof.at[pl.ds(k * depth, depth), :], eof_v.at[pl.ds(k * depth, depth), :], 1 + k)
        for k in range(K_CHUNKS)
    ]
    vec_load = load(vectors, vec_v, 1 + K_CHUNKS)
    energy_load = load(energy, energy_v, 2 + K_CHUNKS)

    tm, space = lax.axis_index("tm"), lax.axis_index("space")
    zh, x = tm >> 2, tm & 3
    y, zl, core = space >> 3, (space >> 1) & 3, space & 1
    z = zh * NZL + zl

    def at(x_, y_, z_, core_):
        return ((z_ & 4) + x_, y_ * 8 + (z_ & 3) * 2 + core_)

    mine = y * 2 + core
    plane = [mine ^ d for d in range(1, 8)]
    plane_peers = [at(x, q >> 1, z, q & 1) for q in plane]
    column_peers = [at(x, y, z ^ d, core) for d in range(1, NZ)]
    xs = [x ^ d for d in range(NX)]
    x_peers = [at(x_, y, z, core) for x_ in xs[1:]]
    y_peers = [at(x, y ^ d, z, core) for d in range(1, NY)]
    other_core = at(x, y, z, core ^ 1)
    far = [(zl + 2) & 7, (zl + 6) & 7]
    far_peers = [[at(x_, y, z_, core) for z_ in far] for x_ in xs]

    barrier = pltpu.get_barrier_semaphore()
    peers = far_peers[2] + far_peers[1] + far_peers[3] + column_peers + plane_peers + x_peers
    for peer in peers:
        pl.semaphore_signal(barrier, inc=1, device_id=peer, device_id_type=MESH)

    def send(source, target, receive, peer, group):
        pltpu.make_async_remote_copy(
            src_ref=source, dst_ref=target, send_sem=sent_sem.at[group], recv_sem=receive,
            device_id=peer, device_id_type=MESH,
        ).start()

    def passed(ref, sem):
        pltpu.make_async_copy(ref, ref, sem).wait()

    def send_snapshots(c):
        for d in range(NX):
            for s in range(2):
                start = pl.multiple_of((xs[d] * 2 + s) * piece + c * width, width)
                send(
                    snap.at[:, pl.ds(start, width)],
                    gathered.at[c, pl.ds(pl.multiple_of(tm * hours, hours), hours), :],
                    snap_sem.at[c], far_peers[d][s], 5 + c,
                )

    snap_load.wait()
    partial = None
    for k in range(K_CHUNKS):
        eof_loads[k].wait()
        term = dot(snap_v[:, k * depth:(k + 1) * depth], eof_v[k * depth:(k + 1) * depth, :])
        partial = term if partial is None else partial + term
    for q in range(8):
        parts[q] = partial[q * 8:(q + 1) * 8, :]

    pl.semaphore_wait(barrier, len(peers))
    send_snapshots(0)

    for q, peer in zip(plane, plane_peers):
        send(parts.at[q], from_plane.at[mine], plane_sem, peer, 0)
    from_plane[mine] = parts[mine]
    vec_load.wait()
    vec_t[...] = vec_v[...].T
    passed(from_plane.at[pl.ds(0, 7)], plane_sem)
    value = from_plane[0]
    for q in range(1, 8):
        value += from_plane[q]

    total[...] = value
    for peer in column_peers:
        send(total, from_column.at[z], column_sem, peer, 1)
    send_snapshots(1)
    from_column[z] = value
    passed(from_column.at[pl.ds(0, 7)], column_sem)
    for h in range(2):
        value = from_column[h * NZL]
        for i in range(1, NZL):
            value += from_column[h * NZL + i]
        coeffs[core, y, x, h] = value

    for peer in x_peers:
        send(coeffs.at[core, y, x], coeffs.at[core, y, x], x_sem, peer, 2)
    send_snapshots(2)
    send_snapshots(3)
    passed(coeffs.at[0, 0, pl.ds(0, 3)], x_sem)
    for peer in y_peers:
        send(coeffs.at[core, y], coeffs.at[core, y], y_sem, peer, 3)
    passed(coeffs.at[0, pl.ds(0, 3)], y_sem)
    send(coeffs.at[core], coeffs.at[core], core_sem, other_core, 4)
    passed(coeffs.at[0], core_sem)

    rows = [
        coeffs[c_, y_, x_, h]
        for h in range(2) for x_ in range(NX) for y_ in range(NY) for c_ in range(NCORE)
    ]
    whole = jnp.concatenate(rows, axis=0)
    first = lax.broadcasted_iota(jnp.int32, whole.shape, 0) == 0
    energy_load.wait()
    scaled = jnp.where(first, 0.0, pltpu.roll(whole, 1, 0)) * energy_v[...]
    scaled_high, scaled_low = two_parts(scaled)
    weights[...] = (
        dot(vec_t[...], scaled_high, ALONG_LAST) + dot(vec_t[...], scaled_low, ALONG_LAST)
    ).astype(BF16)

    owner_zl = (z + 2) & 3
    side = ((z + 6 - owner_zl) & 7) >> 2
    owner_space = y * 8 + owner_zl * 2 + core
    for c in range(CHUNKS):
        passed(gathered.at[c], snap_sem.at[c])
        rebuilt[c] = dot(weights[...], gathered[c]).astype(BF16)
        start = pl.multiple_of((x * 2 + side) * piece + c * width, width)
        for d in range(8):
            to = tm ^ d
            send(
                rebuilt.at[c, pl.ds(pl.multiple_of(to * hours, hours), hours), :],
                modes.at[:, pl.ds(start, width)],
                modes_sem, (to, owner_space), 5 + CHUNKS,
            )

    whole_high, whole_low = two_parts(whole)
    operator[...] = (
        dot(whole_high, scaled_high, ALONG_FIRST)
        + dot(whole_high, scaled_low, ALONG_FIRST)
        + dot(whole_low, scaled_high, ALONG_FIRST)
    )

    passed(parts.at[pl.ds(0, 7)], sent_sem.at[0])
    passed(from_column.at[pl.ds(0, 7)], sent_sem.at[1])
    passed(coeffs.at[0, 0, pl.ds(0, 3)], sent_sem.at[2])
    passed(coeffs.at[0, pl.ds(0, 3)], sent_sem.at[3])
    passed(coeffs.at[0], sent_sem.at[4])
    for c in range(CHUNKS):
        passed(gathered.at[c], sent_sem.at[5 + c])
    passed(rebuilt, sent_sem.at[5 + CHUNKS])
    passed(modes, modes_sem)


def store_kernel(operator, modes, operator_out, modes_out, sems):
    copies = [
        pltpu.make_async_copy(modes, modes_out, sems.at[0]),
        pltpu.make_async_copy(operator, operator_out, sems.at[1]),
    ]
    for copy in copies:
        copy.start()
    for copy in copies:
        copy.wait()


def per_device(eof_basis, snapshots, inverse_energy, eigen_vectors):
    cells, rank = eof_basis.shape
    hours = snapshots.shape[1]
    all_modes = eigen_vectors.shape[1]
    piece = cells // 8
    width = piece // CHUNKS
    anywhere = pl.BlockSpec(memory_space=pl.ANY)
    on_chip = pl.BlockSpec(memory_space=pltpu.VMEM)
    outputs = pl.pallas_call(
        kernel,
        out_shape=(pltpu.VMEM((rank, rank), F32), pltpu.VMEM((hours, cells), BF16)),
        in_specs=[anywhere] * 4,
        out_specs=(on_chip, on_chip),
        scratch_shapes=[
            pltpu.VMEM((cells, rank), BF16),
            pltpu.VMEM((hours, cells), BF16),
            pltpu.VMEM((rank, all_modes), BF16),
            pltpu.VMEM((all_modes, rank), BF16),
            pltpu.VMEM((8, 8, rank), F32),
            pltpu.VMEM((8, 8, rank), F32),
            pltpu.VMEM((NZ, 8, rank), F32),
            pltpu.VMEM((8, rank), F32),
            pltpu.VMEM((NCORE, NY, NX, 2, 8, rank), F32),
            pltpu.VMEM((CHUNKS, 8 * hours, width), BF16),
            pltpu.VMEM((all_modes, 8 * hours), BF16),
            pltpu.VMEM((CHUNKS, all_modes, width), BF16),
            pltpu.VMEM((1, rank), F32),
            pltpu.SemaphoreType.DMA((3 + K_CHUNKS,)),
            pltpu.SemaphoreType.DMA((6 + CHUNKS,)),
            pltpu.SemaphoreType.DMA,
            pltpu.SemaphoreType.DMA,
            pltpu.SemaphoreType.DMA,
            pltpu.SemaphoreType.DMA,
            pltpu.SemaphoreType.DMA,
            pltpu.SemaphoreType.DMA((CHUNKS,)),
            pltpu.SemaphoreType.DMA,
        ],
        compiler_params=pltpu.CompilerParams(
            collective_id=0, has_side_effects=True, vmem_limit_bytes=60 * 1024 * 1024
        ),
    )(eof_basis, snapshots.T, inverse_energy.reshape(1, rank), eigen_vectors)
    return pl.pallas_call(
        store_kernel,
        out_shape=(
            jax.ShapeDtypeStruct((rank, rank), F32),
            jax.ShapeDtypeStruct((hours, cells), BF16),
        ),
        in_specs=[on_chip, on_chip],
        out_specs=(anywhere, anywhere),
        scratch_shapes=[pltpu.SemaphoreType.DMA((2,))],
    )(*[pltpu.with_memory_space_constraint(a, pltpu.VMEM) for a in outputs])


def solution(mesh):
    in_specs = (P("space", None), P("space", "tm"), P(), P())
    out_specs = (P(), P("tm", "space"))
    return jax.shard_map(
        per_device, mesh=mesh, in_specs=in_specs, out_specs=out_specs, check_vma=False
    )
```

time: 65.2 us -> 63.2 us (0.969)
  the two profiles are of different devices: /device:TPU:7 before, /device:TPU:1 now
where the time goes in v2:
time: 63.2 us; the launch traced here: 63.1 us
  Pallas kernels  62.4 us (99%)
  between operations  0.64 us (1%)
    pallas_call x1, Pallas kernels, per_device(): pl.pallas_call(kernel, out_shape=(pltpu.VMEM((rank, rank), F32), pltpu.VM...  61.4 us

profile of v2, /device:TPU:1, one launch (start us, length us, event | category | flops | bytes accessed | tf_op | source)
XLA Modules:
  0.0 63.1 jit_solution(4661781740037782075)
XLA Ops:
  0.6 61.4 %shard_map.59 = (f32[256,256]{1,0:T(8,128)S(1)}, bf16[64,8192]{1,0:T(8,128)(2,1)S(1)}) custom-call(bf16[8192,256]{1,0:T(8,128)(2,1)} %eof.1, bf16[64,8192]{1,0:T(8,128)(2,1)} %bitcast.2, f32[1,256]{1,0:T(1,128)} %bitcast.3, bf16[256,512]{1,0:T(8,128)(2,1)} %vectors.1), custom_call_target="tpu_custom_call" | custom-call | tf_op jit(solution)/shard_map/pallas_call | solution.py:208
  62.0 1.1 %shard_map.60 = (f32[256,256]{1,0:T(8,128)}, bf16[64,8192]{1,0:T(8,128)(2,1)}) custom-call(f32[256,256]{1,0:T(8,128)S(1)} %get-tuple-element.4.operator, bf16[64,8192]{1,0:T(8,128)(2,1)S(1)} %get-tuple-element.5.modes), custom_call_target="tpu_custom_call" | custom-call | tf_op jit(solution)/shard_map/pallas_call | solution.py:241

commit v3 on v2

--- a/solution.py
+++ b/solution.py
@@ -12,7 +12,17 @@
 
 NX, NY, NZ, NZL, NCORE = 4, 4, 8, 4, 2
 CHUNKS = 4
+SAME, CROSS = (0,), (1, 3, 2)
+SCHEDULE = (
+    ((0, SAME),),
+    ((0, CROSS),),
+    ((1, SAME), (1, CROSS)),
+    ((2, SAME), (3, SAME), (2, CROSS), (3, CROSS)),
+)
+SAME_MODES, CROSS_MODES = (0, 4), (1, 5, 3, 7, 2, 6)
+STORES = 4
 K_CHUNKS = 4
+EARLY = 2
 PRODUCT = (((1,), (0,)), ((), ()))
 ALONG_LAST = (((1,), (1,)), ((), ()))
 ALONG_FIRST = (((0,), (0,)), ((), ()))
@@ -31,7 +41,7 @@
     eof, snap, energy, vectors, operator, modes,
     eof_v, snap_v, vec_v, vec_t, parts, from_plane, from_column, total, coeffs,
     gathered, weights, rebuilt, energy_v,
-    load_sem, sent_sem, plane_sem, column_sem, x_sem, y_sem, core_sem,
+    load_sem, sent_sem, word_sem, plane_sem, column_sem, plane_all_sem, core_sem,
     snap_sem, modes_sem,
 ):
     hours, cells = snap.shape
@@ -60,21 +70,25 @@
     def at(x_, y_, z_, core_):
         return ((z_ & 4) + x_, y_ * 8 + (z_ & 3) * 2 + core_)
 
-    mine = y * 2 + core
+    mine, here = y * 2 + core, y * NX + x
     plane = [mine ^ d for d in range(1, 8)]
     plane_peers = [at(x, q >> 1, z, q & 1) for q in plane]
     column_peers = [at(x, y, z ^ d, core) for d in range(1, NZ)]
     xs = [x ^ d for d in range(NX)]
     x_peers = [at(x_, y, z, core) for x_ in xs[1:]]
-    y_peers = [at(x, y ^ d, z, core) for d in range(1, NY)]
+    across_peers = [at(x_, y ^ d, z, core) for d in range(1, NY) for x_ in xs]
     other_core = at(x, y, z, core ^ 1)
     far = [(zl + 2) & 7, (zl + 6) & 7]
     far_peers = [[at(x_, y, z_, core) for z_ in far] for x_ in xs]
+    beside_peers = [at(x, y, (z + d) & 7, core) for d in (1, 7)]
+
+    def tell(semaphore, peers):
+        for peer in peers:
+            pl.semaphore_signal(semaphore, inc=1, device_id=peer, device_id_type=MESH)
 
     barrier = pltpu.get_barrier_semaphore()
-    peers = far_peers[2] + far_peers[1] + far_peers[3] + column_peers + plane_peers + x_peers
-    for peer in peers:
-        pl.semaphore_signal(barrier, inc=1, device_id=peer, device_id_type=MESH)
+    near_peers = far_peers[0] + x_peers + plane_peers + beside_peers
+    tell(barrier, near_peers)
 
     def send(source, target, receive, peer, group):
         pltpu.make_async_remote_copy(
@@ -85,30 +99,38 @@
     def passed(ref, sem):
         pltpu.make_async_copy(ref, ref, sem).wait()
 
-    def send_snapshots(c):
-        for d in range(NX):
-            for s in range(2):
-                start = pl.multiple_of((xs[d] * 2 + s) * piece + c * width, width)
-                send(
-                    snap.at[:, pl.ds(start, width)],
-                    gathered.at[c, pl.ds(pl.multiple_of(tm * hours, hours), hours), :],
-                    snap_sem.at[c], far_peers[d][s], 5 + c,
-                )
+    def send_snapshots(point):
+        for c, offsets in SCHEDULE[point]:
+            for d in offsets:
+                for s in range(2):
+                    start = pl.multiple_of((xs[d] * 2 + s) * piece + c * width, width)
+                    send(
+                        snap.at[:, pl.ds(start, width)],
+                        gathered.at[c, pl.ds(pl.multiple_of(tm * hours, hours), hours), :],
+                        snap_sem.at[c], far_peers[d][s], 4 + c,
+                    )
+
+    def project(k):
+        eof_loads[k].wait()
+        return dot(snap_v[:, k * depth:(k + 1) * depth], eof_v[k * depth:(k + 1) * depth, :])
 
     snap_load.wait()
-    partial = None
-    for k in range(K_CHUNKS):
-        eof_loads[k].wait()
-        term = dot(snap_v[:, k * depth:(k + 1) * depth], eof_v[k * depth:(k + 1) * depth, :])
-        partial = term if partial is None else partial + term
+    partial = project(0)
+    for k in range(1, EARLY):
+        partial += project(k)
+    pl.semaphore_wait(barrier, len(near_peers))
+    tell(word_sem.at[0], x_peers)
+    tell(word_sem.at[1], far_peers[0])
+    send_snapshots(0)
+    for k in range(EARLY, K_CHUNKS):
+        partial += project(k)
     for q in range(8):
         parts[q] = partial[q * 8:(q + 1) * 8, :]
 
-    pl.semaphore_wait(barrier, len(peers))
-    send_snapshots(0)
-
     for q, peer in zip(plane, plane_peers):
         send(parts.at[q], from_plane.at[mine], plane_sem, peer, 0)
+    pl.semaphore_wait(word_sem.at[0], len(x_peers))
+    send_snapshots(1)
     from_plane[mine] = parts[mine]
     vec_load.wait()
     vec_t[...] = vec_v[...].T
@@ -118,30 +140,27 @@
         value += from_plane[q]
 
     total[...] = value
+    pl.semaphore_wait(word_sem.at[1], 2)
     for peer in column_peers:
         send(total, from_column.at[z], column_sem, peer, 1)
-    send_snapshots(1)
+    send_snapshots(2)
     from_column[z] = value
     passed(from_column.at[pl.ds(0, 7)], column_sem)
     for h in range(2):
         value = from_column[h * NZL]
         for i in range(1, NZL):
             value += from_column[h * NZL + i]
-        coeffs[core, y, x, h] = value
-
-    for peer in x_peers:
-        send(coeffs.at[core, y, x], coeffs.at[core, y, x], x_sem, peer, 2)
-    send_snapshots(2)
+        coeffs[core, here, h] = value
+
+    for peer in across_peers + x_peers:
+        send(coeffs.at[core, here], coeffs.at[core, here], plane_all_sem, peer, 2)
     send_snapshots(3)
-    passed(coeffs.at[0, 0, pl.ds(0, 3)], x_sem)
-    for peer in y_peers:
-        send(coeffs.at[core, y], coeffs.at[core, y], y_sem, peer, 3)
-    passed(coeffs.at[0, pl.ds(0, 3)], y_sem)
-    send(coeffs.at[core], coeffs.at[core], core_sem, other_core, 4)
+    passed(coeffs.at[0, pl.ds(0, 15)], plane_all_sem)
+    send(coeffs.at[core], coeffs.at[core], core_sem, other_core, 3)
     passed(coeffs.at[0], core_sem)
 
     rows = [
-        coeffs[c_, y_, x_, h]
+        coeffs[c_, y_ * NX + x_, h]
         for h in range(2) for x_ in range(NX) for y_ in range(NY) for c_ in range(NCORE)
     ]
     whole = jnp.concatenate(rows, axis=0)
@@ -156,17 +175,20 @@
     owner_zl = (z + 2) & 3
     side = ((z + 6 - owner_zl) & 7) >> 2
     owner_space = y * 8 + owner_zl * 2 + core
-    for c in range(CHUNKS):
-        passed(gathered.at[c], snap_sem.at[c])
-        rebuilt[c] = dot(weights[...], gathered[c]).astype(BF16)
+    def send_modes(c, offsets, group):
         start = pl.multiple_of((x * 2 + side) * piece + c * width, width)
-        for d in range(8):
+        for d in offsets:
             to = tm ^ d
             send(
                 rebuilt.at[c, pl.ds(pl.multiple_of(to * hours, hours), hours), :],
                 modes.at[:, pl.ds(start, width)],
-                modes_sem, (to, owner_space), 5 + CHUNKS,
+                modes_sem, (to, owner_space), group,
             )
+
+    for c in range(CHUNKS):
+        passed(gathered.at[c], snap_sem.at[c])
+        rebuilt[c] = dot(weights[...], gathered[c]).astype(BF16)
+        send_modes(c, CROSS_MODES, 4 + CHUNKS + c)
 
     whole_high, whole_low = two_parts(whole)
     operator[...] = (
@@ -175,22 +197,27 @@
         + dot(whole_low, scaled_high, ALONG_FIRST)
     )
 
+    for c in range(CHUNKS):
+        passed(rebuilt.at[c, pl.ds(0, 6 * hours)], sent_sem.at[4 + CHUNKS + c])
+        send_modes(c, SAME_MODES, 4 + 2 * CHUNKS)
+
     passed(parts.at[pl.ds(0, 7)], sent_sem.at[0])
     passed(from_column.at[pl.ds(0, 7)], sent_sem.at[1])
-    passed(coeffs.at[0, 0, pl.ds(0, 3)], sent_sem.at[2])
-    passed(coeffs.at[0, pl.ds(0, 3)], sent_sem.at[3])
-    passed(coeffs.at[0], sent_sem.at[4])
+    passed(coeffs.at[0, pl.ds(0, 15)], sent_sem.at[2])
+    passed(coeffs.at[0], sent_sem.at[3])
     for c in range(CHUNKS):
-        passed(gathered.at[c], sent_sem.at[5 + c])
-    passed(rebuilt, sent_sem.at[5 + CHUNKS])
+        passed(gathered.at[c], sent_sem.at[4 + c])
+    passed(rebuilt.at[:, pl.ds(0, 2 * hours)], sent_sem.at[4 + 2 * CHUNKS])
     passed(modes, modes_sem)
 
 
 def store_kernel(operator, modes, operator_out, modes_out, sems):
+    step = modes.shape[1] // STORES
     copies = [
-        pltpu.make_async_copy(modes, modes_out, sems.at[0]),
-        pltpu.make_async_copy(operator, operator_out, sems.at[1]),
+        pltpu.make_async_copy(modes.at[:, pl.ds(i * step, step)], modes_out.at[:, pl.ds(i * step, step)], sems.at[i])
+        for i in range(STORES)
     ]
+    copies.append(pltpu.make_async_copy(operator, operator_out, sems.at[STORES]))
     for copy in copies:
         copy.start()
     for copy in copies:
@@ -219,14 +246,14 @@
             pltpu.VMEM((8, 8, rank), F32),
             pltpu.VMEM((NZ, 8, rank), F32),
             pltpu.VMEM((8, rank), F32),
-            pltpu.VMEM((NCORE, NY, NX, 2, 8, rank), F32),
+            pltpu.VMEM((NCORE, NY * NX, 2, 8, rank), F32),
             pltpu.VMEM((CHUNKS, 8 * hours, width), BF16),
             pltpu.VMEM((all_modes, 8 * hours), BF16),
             pltpu.VMEM((CHUNKS, all_modes, width), BF16),
             pltpu.VMEM((1, rank), F32),
             pltpu.SemaphoreType.DMA((3 + K_CHUNKS,)),
-            pltpu.SemaphoreType.DMA((6 + CHUNKS,)),
-            pltpu.SemaphoreType.DMA,
+            pltpu.SemaphoreType.DMA((5 + 2 * CHUNKS,)),
+            pltpu.SemaphoreType.REGULAR((2,)),
             pltpu.SemaphoreType.DMA,
             pltpu.SemaphoreType.DMA,
             pltpu.SemaphoreType.DMA,
@@ -246,7 +273,7 @@
         ),
         in_specs=[on_chip, on_chip],
         out_specs=(anywhere, anywhere),
-        scratch_shapes=[pltpu.SemaphoreType.DMA((2,))],
+        scratch_shapes=[pltpu.SemaphoreType.DMA((STORES + 1,))],
     )(*[pltpu.with_memory_space_constraint(a, pltpu.VMEM) for a in outputs])
 
 

time: 63.2 us -> 60.9 us (0.964)
  Pallas kernels: 62.4 us -> 60.1 us
    pallas_call x1, Pallas kernels: 61.4 us -> 59 us  [per_device(): pl.pallas_call(kernel, out_shape=(pltpu.VMEM((rank, rank), F32), pltpu.VM...]
where the time goes in v3:
time: 60.9 us; the launch traced here: 60.8 us
  Pallas kernels  60.1 us (99%)
  between operations  0.64 us (1%)
    pallas_call x1, Pallas kernels, per_device(): pl.pallas_call(kernel, out_shape=(pltpu.VMEM((rank, rank), F32), pltpu.VM...  59 us

profile of v3, /device:TPU:1, one launch (start us, length us, event | category | flops | bytes accessed | tf_op | source)
XLA Modules:
  0.0 60.8 jit_solution(5791480951863911080)
XLA Ops:
  0.6 59.0 %shard_map.59 = (f32[256,256]{1,0:T(8,128)S(1)}, bf16[64,8192]{1,0:T(8,128)(2,1)S(1)}) custom-call(bf16[8192,256]{1,0:T(8,128)(2,1)} %eof.1, bf16[64,8192]{1,0:T(8,128)(2,1)} %bitcast.2, f32[1,256]{1,0:T(1,128)} %bitcast.3, bf16[256,512]{1,0:T(8,128)(2,1)} %vectors.1), custom_call_target="tpu_custom_call" | custom-call | tf_op jit(solution)/shard_map/pallas_call | solution.py:235
  59.7 1.1 %shard_map.60 = (f32[256,256]{1,0:T(8,128)}, bf16[64,8192]{1,0:T(8,128)(2,1)}) custom-call(f32[256,256]{1,0:T(8,128)S(1)} %get-tuple-element.4.operator, bf16[64,8192]{1,0:T(8,128)(2,1)S(1)} %get-tuple-element.5.modes), custom_call_target="tpu_custom_call" | custom-call | tf_op jit(solution)/shard_map/pallas_call | solution.py:268

commit v4 on v3

--- a/solution.py
+++ b/solution.py
@@ -15,9 +15,9 @@
 SAME, CROSS = (0,), (1, 3, 2)
 SCHEDULE = (
     ((0, SAME),),
-    ((0, CROSS),),
-    ((1, SAME), (1, CROSS)),
-    ((2, SAME), (3, SAME), (2, CROSS), (3, CROSS)),
+    ((0, CROSS), (1, SAME)),
+    ((1, CROSS), (2, SAME)),
+    ((3, SAME), (2, CROSS), (3, CROSS)),
 )
 SAME_MODES, CROSS_MODES = (0, 4), (1, 5, 3, 7, 2, 6)
 STORES = 4
@@ -105,7 +105,7 @@
                 for s in range(2):
                     start = pl.multiple_of((xs[d] * 2 + s) * piece + c * width, width)
                     send(
-                        snap.at[:, pl.ds(start, width)],
+                        snap_v.at[:, pl.ds(start, width)],
                         gathered.at[c, pl.ds(pl.multiple_of(tm * hours, hours), hours), :],
                         snap_sem.at[c], far_peers[d][s], 4 + c,
                     )

time: 60.9 us -> 60.4 us (level)
  no operation moved by 1% of the time
where the time goes in v4:
time: 60.4 us; the launch traced here: 60.3 us
  Pallas kernels  59.7 us (99%)
  between operations  0.64 us (1%)
    pallas_call x1, Pallas kernels, per_device(): pl.pallas_call(kernel, out_shape=(pltpu.VMEM((rank, rank), F32), pltpu.VM...  58.6 us

profile of v4, /device:TPU:1, one launch (start us, length us, event | category | flops | bytes accessed | tf_op | source)
XLA Modules:
  0.0 60.3 jit_solution(14752424548911650449)
XLA Ops:
  0.6 58.6 %shard_map.59 = (f32[256,256]{1,0:T(8,128)S(1)}, bf16[64,8192]{1,0:T(8,128)(2,1)S(1)}) custom-call(bf16[8192,256]{1,0:T(8,128)(2,1)} %eof.1, bf16[64,8192]{1,0:T(8,128)(2,1)} %bitcast.2, f32[1,256]{1,0:T(1,128)} %bitcast.3, bf16[256,512]{1,0:T(8,128)(2,1)} %vectors.1), custom_call_target="tpu_custom_call" | custom-call | tf_op jit(solution)/shard_map/pallas_call | solution.py:235
  59.2 1.1 %shard_map.60 = (f32[256,256]{1,0:T(8,128)}, bf16[64,8192]{1,0:T(8,128)(2,1)}) custom-call(f32[256,256]{1,0:T(8,128)S(1)} %get-tuple-element.4.operator, bf16[64,8192]{1,0:T(8,128)(2,1)S(1)} %get-tuple-element.5.modes), custom_call_target="tpu_custom_call" | custom-call | tf_op jit(solution)/shard_map/pallas_call | solution.py:268

commit v5 on v4

--- a/solution.py
+++ b/solution.py
@@ -73,7 +73,7 @@
     mine, here = y * 2 + core, y * NX + x
     plane = [mine ^ d for d in range(1, 8)]
     plane_peers = [at(x, q >> 1, z, q & 1) for q in plane]
-    column_peers = [at(x, y, z ^ d, core) for d in range(1, NZ)]
+    column_peers = [at(x, y, z ^ d, core) for d in (4, 5, 3, 7, 2, 6, 1)]
     xs = [x ^ d for d in range(NX)]
     x_peers = [at(x_, y, z, core) for x_ in xs[1:]]
     across_peers = [at(x_, y ^ d, z, core) for d in range(1, NY) for x_ in xs]
@@ -175,6 +175,7 @@
     owner_zl = (z + 2) & 3
     side = ((z + 6 - owner_zl) & 7) >> 2
     owner_space = y * 8 + owner_zl * 2 + core
+
     def send_modes(c, offsets, group):
         start = pl.multiple_of((x * 2 + side) * piece + c * width, width)
         for d in offsets:

time: 60.4 us -> 60.3 us (level)
  no operation moved by 1% of the time
where the time goes in v5:
time: 60.3 us; the launch traced here: 60.2 us
  Pallas kernels  59.6 us (99%)
  between operations  0.64 us (1%)
    pallas_call x1, Pallas kernels, per_device(): pl.pallas_call(kernel, out_shape=(pltpu.VMEM((rank, rank), F32), pltpu.VM...  58.5 us

profile of v5, /device:TPU:1, one launch (start us, length us, event | category | flops | bytes accessed | tf_op | source)
XLA Modules:
  0.0 60.2 jit_solution(2691690106740220375)
XLA Ops:
  0.6 58.5 %shard_map.59 = (f32[256,256]{1,0:T(8,128)S(1)}, bf16[64,8192]{1,0:T(8,128)(2,1)S(1)}) custom-call(bf16[8192,256]{1,0:T(8,128)(2,1)} %eof.1, bf16[64,8192]{1,0:T(8,128)(2,1)} %bitcast.2, f32[1,256]{1,0:T(1,128)} %bitcast.3, bf16[256,512]{1,0:T(8,128)(2,1)} %vectors.1), custom_call_target="tpu_custom_call" | custom-call | tf_op jit(solution)/shard_map/pallas_call | solution.py:236
  59.1 1.1 %shard_map.60 = (f32[256,256]{1,0:T(8,128)}, bf16[64,8192]{1,0:T(8,128)(2,1)}) custom-call(f32[256,256]{1,0:T(8,128)S(1)} %get-tuple-element.4.operator, bf16[64,8192]{1,0:T(8,128)(2,1)S(1)} %get-tuple-element.5.modes), custom_call_target="tpu_custom_call" | custom-call | tf_op jit(solution)/shard_map/pallas_call | solution.py:269

commit v6 on v5

--- a/solution.py
+++ b/solution.py
@@ -16,8 +16,9 @@
 SCHEDULE = (
     ((0, SAME),),
     ((0, CROSS), (1, SAME)),
-    ((1, CROSS), (2, SAME)),
-    ((3, SAME), (2, CROSS), (3, CROSS)),
+    ((1, CROSS),),
+    ((2, CROSS), (3, CROSS)),
+    ((2, SAME), (3, SAME)),
 )
 SAME_MODES, CROSS_MODES = (0, 4), (1, 5, 3, 7, 2, 6)
 STORES = 4
@@ -145,6 +146,8 @@
         send(total, from_column.at[z], column_sem, peer, 1)
     send_snapshots(2)
     from_column[z] = value
+    passed(gathered.at[0], sent_sem.at[4])
+    send_snapshots(4)
     passed(from_column.at[pl.ds(0, 7)], column_sem)
     for h in range(2):
         value = from_column[h * NZL]
@@ -206,7 +209,7 @@
     passed(from_column.at[pl.ds(0, 7)], sent_sem.at[1])
     passed(coeffs.at[0, pl.ds(0, 15)], sent_sem.at[2])
     passed(coeffs.at[0], sent_sem.at[3])
-    for c in range(CHUNKS):
+    for c in range(1, CHUNKS):
         passed(gathered.at[c], sent_sem.at[4 + c])
     passed(rebuilt.at[:, pl.ds(0, 2 * hours)], sent_sem.at[4 + 2 * CHUNKS])
     passed(modes, modes_sem)

time: 60.3 us -> 60.3 us (level)
  no operation moved by 1% of the time
where the time goes in v6:
time: 60.3 us; the launch traced here: 60.2 us
  Pallas kernels  59.6 us (99%)
  between operations  0.64 us (1%)
    pallas_call x1, Pallas kernels, per_device(): pl.pallas_call(kernel, out_shape=(pltpu.VMEM((rank, rank), F32), pltpu.VM...  58.5 us

profile of v6, /device:TPU:1, one launch (start us, length us, event | category | flops | bytes accessed | tf_op | source)
XLA Modules:
  0.0 60.2 jit_solution(2780025150397253699)
XLA Ops:
  0.6 58.5 %shard_map.59 = (f32[256,256]{1,0:T(8,128)S(1)}, bf16[64,8192]{1,0:T(8,128)(2,1)S(1)}) custom-call(bf16[8192,256]{1,0:T(8,128)(2,1)} %eof.1, bf16[64,8192]{1,0:T(8,128)(2,1)} %bitcast.2, f32[1,256]{1,0:T(1,128)} %bitcast.3, bf16[256,512]{1,0:T(8,128)(2,1)} %vectors.1), custom_call_target="tpu_custom_call" | custom-call | tf_op jit(solution)/shard_map/pallas_call | solution.py:239
  59.1 1.1 %shard_map.60 = (f32[256,256]{1,0:T(8,128)}, bf16[64,8192]{1,0:T(8,128)(2,1)}) custom-call(f32[256,256]{1,0:T(8,128)S(1)} %get-tuple-element.4.operator, bf16[64,8192]{1,0:T(8,128)(2,1)S(1)} %get-tuple-element.5.modes), custom_call_target="tpu_custom_call" | custom-call | tf_op jit(solution)/shard_map/pallas_call | solution.py:272
